TPU v7x, 512 devices: a whole 4x8x8 slice. The times are simulated.
512 devices in a mesh: section: 2 (over core), sy: 8 (over y), sx: 8 (over z), mb: 4 (over x).
Axes of the slice: x: 4, y: 8, z: 8, core: 2. Of those that a mesh axis runs over, the one named last changes fastest.
Arguments:
- frames: bfloat16 [4, 512, 512, 128], P('mb', 'sy', 'sx'), may hold values from -6 to 6
- encode_weight: bfloat16 [512, 384], replicated, may hold values from -0.25 to 0.25
- conv_weight: bfloat16 [2, 1, 3456, 384], P('section', None, ('sy', 'sx')), may hold values from -0.109375 to 0.109375
- norm_gain: float32 [2, 1, 384], P('section'), may hold values from 0.1 to 1.9
- head_weight: bfloat16 [384, 256], replicated, may hold values from -0.3125 to 0.3125
- prior_logits: bfloat16 [4, 256, 256, 256], P('mb', 'sy', 'sx'), may hold values from -12 to 249
- target_bins: int32 [4, 256, 256], P('mb', 'sy', 'sx'), may hold values from 0 to 255
Outputs:
- section_features: bfloat16 [2, 4, 256, 256, 384], P('section', 'mb', 'sy', 'sx')
- head_step: float32 [384, 256], P('section')
- mean_loss: float32 [], replicated
All inputs are finite; a program needn't handle non-finite values.
Results may differ from a plain program's by a relative error of at most 0.008.
Values may be sent and summed in bfloat16 or wider, within the bound.
No kernel may reach another device: no remote copies, remote signals or barrier semaphores. Data moves between devices by JAX's collectives and lax.ppermute only.
A program may use at most 64 MiB of HBM per device.

v0:
```python
import jax
import jax.numpy as jnp
from jax import lax
from jax.sharding import PartitionSpec as P

FIRST_DILATION = 1


def padded_2(block, sides, width):
    for axis, dim in sides:
        count = lax.axis_size(axis)
        forward = [(i, i + 1) for i in range(count - 1)]
        backward = [(target, source) for source, target in forward]
        low = lax.ppermute(
            lax.slice_in_dim(block, block.shape[dim] - width, None, axis=dim), axis, forward
        )
        high = lax.ppermute(lax.slice_in_dim(block, 0, width, axis=dim), axis, backward)
        block = jnp.concatenate([low, block, high], axis=dim)
    return block


def from_behind(block, axis, distance):
    devices = range(lax.axis_size(axis))
    route = [(i - distance, i) for i in devices if i - distance in devices]
    return lax.ppermute(block, axis, route)


def norm_gelu(activations, gain):
    values = activations.astype(jnp.float32)
    center = jnp.mean(values, axis=-1, keepdims=True)
    offset = values - center
    spread = jnp.mean(offset * offset, axis=-1, keepdims=True)
    normed = offset * lax.rsqrt(spread + 1e-05) * gain
    return jax.nn.gelu(normed, approximate=False).astype(jnp.bfloat16)


def per_device(
    frames, encode_weight, conv_weight, norm_gain, head_weight, prior_logits, target_bins
):
    first_section = lax.axis_index("section") == 0
    micro_count = frames.shape[0]
    side_cells = frames.shape[1] // 2
    input_width = frames.shape[3]
    channels = encode_weight.shape[1]
    bins_count = head_weight.shape[1]
    parts_y = lax.axis_size("sy")
    parts_x = lax.axis_size("sx")
    cell_count = side_cells * side_cells
    kernel = encode_weight.reshape(2, 2, input_width, channels)
    grad_total = jnp.zeros((channels, bins_count), jnp.float32)
    loss_total = jnp.zeros((), jnp.float32)
    first_out = []
    second_out = []
    handed = None
    for tick_index in range(micro_count + 1):
        if tick_index == 0:
            blocks = frames[0].reshape(side_cells, 2, side_cells, 2, input_width)
            activations = jnp.einsum(
                "apbqc,pqco->abo", blocks, kernel, preferred_element_type=jnp.float32
            ).astype(jnp.bfloat16)
        else:
            activations = handed
        apply_reach = FIRST_DILATION * 2**0
        hidden = norm_gelu(activations, norm_gain[0, 0])
        haloed = padded_2(hidden, (("sy", 0), ("sx", 1)), apply_reach)
        zero_padded = jnp.pad(
            hidden, ((apply_reach, apply_reach), (apply_reach, apply_reach), (0, 0))
        )
        apply_padded = jnp.where(first_section, haloed, zero_padded)
        windows = [
            apply_padded[
                tap_row * apply_reach : tap_row * apply_reach + side_cells,
                tap_column * apply_reach : tap_column * apply_reach + side_cells,
            ]
            for tap_row in range(3)
            for tap_column in range(3)
        ]
        patches = jnp.concatenate(windows, axis=2).reshape(cell_count, 9 * channels)
        summed = jnp.dot(
            patches,
            lax.all_gather(conv_weight[0, 0], ("sy", "sx"), axis=0, tiled=True),
            preferred_element_type=jnp.float32,
        )
        activations = (
            activations.astype(jnp.float32) + summed.reshape(side_cells, side_cells, channels)
        ).astype(jnp.bfloat16)
        if tick_index < micro_count:
            first_out.append(activations)
        rows_y = side_cells // parts_y
        rows_x = side_cells // parts_x
        plain_view = activations.reshape(parts_y, rows_y, parts_x, rows_x, channels)
        spaced = activations.reshape(rows_y, parts_y, rows_x, parts_x, channels).transpose(
            1, 0, 3, 2, 4
        )
        outgoing = jnp.where(first_section, spaced, plain_view)
        arrived = lax.all_to_all(
            lax.all_to_all(outgoing, "sy", split_axis=0, concat_axis=0, tiled=True),
            "sx",
            split_axis=2,
            concat_axis=2,
            tiled=True,
        )
        direct = arrived.reshape(side_cells, side_cells, channels)
        restored = arrived.transpose(1, 0, 3, 2, 4).reshape(side_cells, side_cells, channels)
        moved = jnp.where(first_section, direct, restored)
        if tick_index >= 1:
            second_out.append(moved)
            flat_rows = moved.reshape(cell_count, channels)
            logits = jnp.dot(flat_rows, head_weight, preferred_element_type=jnp.float32)
            logits = logits + prior_logits[tick_index - 1].reshape(cell_count, bins_count).astype(
                jnp.float32
            )
            row_top = jnp.max(logits, axis=1, keepdims=True)
            shifted = logits - row_top
            exp_terms = jnp.exp(shifted)
            exp_total = jnp.sum(exp_terms, axis=1, keepdims=True)
            softmax_rows = exp_terms / exp_total
            onehot = (
                target_bins[tick_index - 1].reshape(cell_count, 1)
                == lax.broadcasted_iota(jnp.int32, (1, bins_count), 1)
            ).astype(jnp.float32)
            loss_sum = jnp.sum(jnp.log(exp_total[:, 0]) - jnp.sum(shifted * onehot, axis=1))
            delta_rows = (softmax_rows - onehot).astype(jnp.bfloat16)
            grad_part = lax.dot_general(
                flat_rows, delta_rows, (((0,), (0,)), ((), ())), preferred_element_type=jnp.float32
            )
            grad_part, loss_sum = (grad_part, loss_sum)
            grad_total = jnp.where(first_section, 0.0, grad_part)
            loss_total = jnp.where(first_section, 0.0, loss_sum)
        if tick_index < micro_count:
            handed = from_behind(moved, "section", 1)
    stacked = jnp.stack([jnp.where(first_section, first_out[0], second_out[0])])[None]
    gradient, loss_all = lax.psum((grad_total, loss_total), ("sy", "sx", "mb"))
    head_full = gradient * lax.rsqrt(jnp.mean(gradient * gradient) + 1e-06)
    mean_local = loss_all / (micro_count * lax.axis_size("mb") * cell_count * parts_y * parts_x)
    half_rows = channels // 2
    sent_rows, sent_loss = (
        from_behind(head_full[:half_rows].astype(jnp.bfloat16), "section", -1).astype(jnp.float32),
        from_behind(mean_local.astype(jnp.bfloat16), "section", -1).astype(mean_local.dtype),
    )
    head_step = jnp.where(first_section, sent_rows, head_full[half_rows:])
    mean_loss = jnp.where(first_section, sent_loss, mean_local)
    return (stacked, head_step, mean_loss)


def solution(mesh):
    placed = (
        P("mb", "sy", "sx", None),
        P(),
        P("section", None, ("sy", "sx"), None),
        P("section", None, None),
        P(),
        P("mb", "sy", "sx", None),
        P("mb", "sy", "sx"),
    )
    return jax.shard_map(
        per_device,
        mesh=mesh,
        in_specs=placed,
        out_specs=(P("section", "mb", "sy", "sx", None), P("section", None), P()),
        check_vma=False,
    )
```

profile of v0, /device:TPU:1, one launch (start us, length us, event | category | flops | bytes accessed | tf_op | source)
XLA Modules:
  0.0 957.4 jit_solution(2720262242174057233)
XLA Ops:
  7.2 1.5 copy.50
  9.5 2.0 convert_reduce_fusion.1
  12.0 3.8 fusion.20
  15.9 4.0 collective-permute-start
  21.2 3.3 collective-permute-done.1
  24.6 4.0 collective-permute-start.2
  29.9 4.2 collective-permute-done.3
  45.5 57.8 %all-gather.3.cloned.1.call-done = bf16[1,1,3456,384]{3,1,0,2:T(2,128)(2,1)} async-done(((bf16[1,1,54,384]{3,1,0,2:T(2,128)(2,1)}), bf16[1,1,3456,384]{3,1,0,2:T(2,128)(2,1)}) %all-gather.3.cloned.1.call-update) | async-done | bytes 2654224 | tf_op jit(solution)/shard_map/all_gather | solution.py:81
  103.3 8.4 fusion.22
  112.4 23.7 %all_to_all.20 = bf16[8,4,8,4,384]{4,3,1,2,0:T(4,128)(2,1)S(1)} all-to-all(bf16[8,4,8,4,384]{4,3,1,2,0:T(4,128)(2,1)S(1)} %bitcast_select_fusion.2), channel_id=1, replica_groups=mesh['section'=2,'sy'=8,'sx'=8,'mb'=4] {'sy'}, dimensions={0} | all-to-all | bytes 1572864 | tf_op jit(solution)/shard_map/all_to_all | solution.py:97
  136.3 19.7 %all_to_all.21 = bf16[8,4,8,4,384]{4,3,1,0,2:T(4,128)(2,1)S(1)} all-to-all(bf16[8,4,8,4,384]{4,3,1,0,2:T(4,128)(2,1)S(1)} %copy.53), channel_id=1, replica_groups=mesh['section'=2,'sy'=8,'sx'=8,'mb'=4] {'sx'}, dimensions={2} | all-to-all | bytes 1572864 | tf_op jit(solution)/shard_map/all_to_all | solution.py:96
  157.3 1.5 collective-permute-start.4
  158.8 9.2 collective-permute-done.4
  168.8 3.8 fusion.13
  175.3 3.3 collective-permute-done.6
  178.7 2.2 collective-permute-start.7
  182.2 3.6 collective-permute-done.8
  189.1 3.9 fusion.24
  193.6 24.2 %all_to_all.22 = bf16[8,4,8,4,384]{4,3,1,2,0:T(4,128)(2,1)S(1)} all-to-all(bf16[8,4,8,4,384]{4,3,1,2,0:T(4,128)(2,1)S(1)} %bitcast_select_fusion.1), channel_id=1, replica_groups=mesh['section'=2,'sy'=8,'sx'=8,'mb'=4] {'sy'}, dimensions={0} | all-to-all | bytes 1572864 | tf_op jit(solution)/shard_map/all_to_all | solution.py:97
  219.0 3.5 all-to-all-start.3
  225.1 16.5 %all-to-all-done.3 = bf16[8,4,8,4,384]{4,3,1,0,2:T(4,128)(2,1)S(1)} async-done(((bf16[8,4,8,4,384]{4,3,1,0,2:T(4,128)(2,1)}), bf16[8,4,8,4,384]{4,3,1,0,2:T(4,128)(2,1)S(1)}, u32[]{:S(2)}, u32[]{:S(2)}) %all-to-all-start.3) | async-done | bytes 786464 | tf_op jit(solution)/shard_map/all_to_all | solution.py:96
  248.7 575.3 %psum.15 = f32[]{:T(128)} all-reduce(f32[]{:T(128)S(6)} %select_n.85), channel_id=1, replica_groups=mesh['section'=2,'sy'=8,'sx'=8,'mb'=4] {'sy','sx','mb'}, use_global_device_ids=true, to_apply=%region_10.11 | all-reduce | flops 1 | bytes 8 | tf_op jit(solution)/shard_map/psum | solution.py:133
  824.8 117.5 %collective-permute-start.10 = (bf16[]{:T(256)}, bf16[]{:T(256)}, u32[]{:S(2)}, u32[]{:S(2)}) collective-permute-start(bf16[]{:T(256)} %convert_element_type.60), channel_id=1, source_target_pairs={{256,0},{257,1},{258,2},{259,3},{260,4},{261,5},{262,6},{263,7},{2... | collective-permute-start | bytes 14 | tf_op jit(solution)/shard_map/ppermute | solution.py:25
  942.3 1.7 multiply_reduce_fusion
  (90 shorter events, 40.6 us)
Async XLA Ops:
  7.2 2.3 copy-start
  7.2 96.1 %all-gather.3.cloned.1.call-start = ((), (), s32[]{:S(2)}) async-start(), calls=%async_computation.5 | async-start | bytes 5391360 | tf_op jit(solution)/shard_map/all_gather | solution.py:81
  15.9 5.3 collective-permute-start
  19.9 4.6 collective-permute-start.1
  24.6 5.3 collective-permute-start.2
  28.6 5.5 collective-permute-start.3
  157.3 10.7 %collective-permute-start.4 = (bf16[32,32,384]{2,1,0:T(8,128)(2,1)S(1)}, bf16[32,32,384]{2,1,0:T(8,128)(2,1)S(1)}, u32[]{:S(2)}, u32[]{:S(2)}) collective-permute-start(bf16[32,32,384]{2,1,0:T(8,128)(2,1)S(1)} %broadcast_select_fusion), channel_id=1, source_target_pairs={{0,256},{1,257},{2,258},{3,259},{4,260},{5,261},{6,262},{7,263},{8... | collective-permute-start | bytes 2359304 | tf_op jit(solution)/shard_map/ppermute | solution.py:25
  172.6 2.7 collective-permute-start.5
  174.0 4.6 collective-permute-start.6
  178.7 3.5 collective-permute-start.7
  180.9 4.9 collective-permute-start.8
  186.3 2.8 slice-start
  187.4 1.7 slice-start.1
  217.8 5.0 copy-start.3
  219.0 22.6 %all-to-all-start.3 = ((bf16[8,4,8,4,384]{4,3,1,0,2:T(4,128)(2,1)}), bf16[8,4,8,4,384]{4,3,1,0,2:T(4,128)(2,1)S(1)}, u32[]{:S(2)}, u32[]{:S(2)}) async-start(bf16[8,4,8,4,384]{4,3,1,0,2:T(4,128)(2,1)} %copy.58), calls=%async_computation.3 | async-start | bytes 1572864 | tf_op jit(solution)/shard_map/all_to_all | solution.py:96
  222.5 719.8 %all-reduce.4.cloned.1.call-start = ((), (), s32[]{:S(2)}) async-start(), calls=%async_computation.4 | async-start | bytes 786432 | tf_op jit(solution)/shard_map/psum | solution.py:133
  243.0 1.1 copy-start.2
  244.1 1.2 copy-start.1
  244.1 1.2 copy-start.4
  824.8 123.2 %collective-permute-start.10 = (bf16[]{:T(256)}, bf16[]{:T(256)}, u32[]{:S(2)}, u32[]{:S(2)}) collective-permute-start(bf16[]{:T(256)} %convert_element_type.60), channel_id=1, source_target_pairs={{256,0},{257,1},{258,2},{259,3},{260,4},{261,5},{262,6},{263,7},{2... | collective-permute-start | bytes 14 | tf_op jit(solution)/shard_map/ppermute | solution.py:25
  945.7 2.9 collective-permute-start.9
Sparse Core Ops, SparseCore 0:
  11.7 91.6 all-gather.2
  247.5 225.9 all-reduce.3
where the time goes:
time: 958 us; the launch traced here: 957 us
  blocking collectives  643 us (67%)
  starting transfers between devices  141 us (15%)
  waiting for transfers between devices  97.9 us (10%)
  local copies, waits for them, and re-layouts  24 us (3%)
  between operations  18.2 us (2%)
  other arithmetic  17.5 us (2%)
  matrix products  16.1 us (2%)
    psum x1, blocking collectives, per_device(): gradient, loss_all = lax.psum((grad_total, loss_total), ('sy', 'sx', 'mb'))  575 us
    ppermute x3, starting transfers between devices, from_behind(): return lax.ppermute(block, axis, route)  120 us
    all_gather x1, waiting for transfers between devices, per_device(): lax.all_gather(conv_weight[0, 0], ('sy', 'sx'), axis=0, tiled=True)  57.8 us
    all_to_all x2, blocking collectives, per_device(): lax.all_to_all(outgoing, 'sy', split_axis=0, concat_axis=0, tiled=True)  47.8 us
    all_to_all x1, blocking collectives, per_device(): lax.all_to_all(lax.all_to_all(outgoing, 'sy', split_axis=0, concat_axis=0...  19.7 us
  transfers between devices with their start and end apart: 14, of which 7 were waited for; matrix products, arithmetic and copies ran while one was open for 3% of the time, Pallas kernels for 0%

commit v1 on v0

--- a/solution.py
+++ b/solution.py
@@ -130,7 +130,7 @@
         if tick_index < micro_count:
             handed = from_behind(moved, "section", 1)
     stacked = jnp.stack([jnp.where(first_section, first_out[0], second_out[0])])[None]
-    gradient, loss_all = lax.psum((grad_total, loss_total), ("sy", "sx", "mb"))
+    gradient, loss_all = lax.psum(lax.psum((grad_total, loss_total), ("sx", "mb")), "sy")
     head_full = gradient * lax.rsqrt(jnp.mean(gradient * gradient) + 1e-06)
     mean_local = loss_all / (micro_count * lax.axis_size("mb") * cell_count * parts_y * parts_x)
     half_rows = channels // 2

time: 958 us -> 514 us (0.54)
  blocking collectives: 643 us -> 141 us
  waiting for transfers between devices: 97.9 us -> 247 us
  starting transfers between devices: 141 us -> 48.3 us
    psum x1 -> x2, blocking collectives: 575 us -> 73.4 us  [the longest x1 58.8 us: per_device(): lax.psum((grad_total, loss_total), ('sx', 'mb'))]
    psum x1 -> x2, waiting for transfers between devices: 0.01 us -> 150 us  [the longest x1 150 us: per_device(): lax.psum((grad_total, loss_total), ('sx', 'mb'))]
    ppermute x3, starting transfers between devices: 120 us -> 27.7 us  [from_behind(): return lax.ppermute(block, axis, route)]
  transfers between devices with their start and end apart: 14 -> 15, of which waited for: 7 -> 8; matrix products, arithmetic and copies ran while one was open for 3% -> 5% of each run, Pallas kernels for 0% -> 0%
where the time goes in v1:
time: 514 us; the launch traced here: 513 us
  waiting for transfers between devices  247 us (48%)
  blocking collectives  141 us (27%)
  starting transfers between devices  48.3 us (9%)
  local copies, waits for them, and re-layouts  24.6 us (5%)
  other arithmetic  18.4 us (4%)
  between operations  18 us (4%)
  matrix products  16 us (3%)
    psum x1, waiting for transfers between devices, per_device(): lax.psum((grad_total, loss_total), ('sx', 'mb'))  150 us
    psum x1, blocking collectives, per_device(): lax.psum((grad_total, loss_total), ('sx', 'mb'))  58.8 us
    all_gather x1, waiting for transfers between devices, per_device(): lax.all_gather(conv_weight[0, 0], ('sy', 'sx'), axis=0, tiled=True)  57.8 us
    all_to_all x2, blocking collectives, per_device(): lax.all_to_all(outgoing, 'sy', split_axis=0, concat_axis=0, tiled=True)  47.8 us
    ppermute x3, starting transfers between devices, from_behind(): return lax.ppermute(block, axis, route)  27.7 us
    all_to_all x1, blocking collectives, per_device(): lax.all_to_all(lax.all_to_all(outgoing, 'sy', split_axis=0, concat_axis=0...  19.7 us
    all_to_all x1, waiting for transfers between devices, per_device(): lax.all_to_all(lax.all_to_all(outgoing, 'sy', split_axis=0, concat_axis=0...  15 us
    unnamed x33, local copies, waits for them, and re-layouts  15 us
  transfers between devices with their start and end apart: 15, of which 8 were waited for; matrix products, arithmetic and copies ran while one was open for 5% of the time, Pallas kernels for 0%

profile of v1, /device:TPU:1, one launch (start us, length us, event | category | flops | bytes accessed | tf_op | source)
XLA Modules:
  0.0 513.0 jit_solution(13120472401288651312)
XLA Ops:
  9.5 2.0 convert_reduce_fusion.1
  12.0 3.8 fusion.20
  15.8 4.0 collective-permute-start
  21.2 3.3 collective-permute-done.1
  24.5 4.0 collective-permute-start.2
  29.9 4.2 collective-permute-done.3
  45.5 57.8 %all-gather.3.cloned.1.call-done = bf16[1,1,3456,384]{3,1,0,2:T(2,128)(2,1)} async-done(((bf16[1,1,54,384]{3,1,0,2:T(2,128)(2,1)}), bf16[1,1,3456,384]{3,1,0,2:T(2,128)(2,1)}) %all-gather.3.cloned.1.call-update) | async-done | bytes 2654224 | tf_op jit(solution)/shard_map/all_gather | solution.py:81
  103.3 8.4 %fusion.22 = bf16[32,32,384]{2,1,0:T(8,128)(2,1)S(1)} fusion(bf16[32,32,384]{2,1,0:T(8,128)(2,1)S(1)} %get-tuple-element.14, bf16[32,32,3456]{2,1,0:T(8,128)(2,1)} %slice_dynamic-update-slice_fusion.9, bf16[1,1,3456,384]{3,1,0,2:T(2,128)(2,1)} %all-gather.3.cloned.1.call-done), kind=kOutput, calls=%fused_computation.30 | convolution fusion | flops 2719088640 | bytes 11304960 | tf_op jit(solution)/shard_map/dot_general | solution.py:79
  112.3 23.7 %all_to_all.20 = bf16[8,4,8,4,384]{4,3,1,2,0:T(4,128)(2,1)S(1)} all-to-all(bf16[8,4,8,4,384]{4,3,1,2,0:T(4,128)(2,1)S(1)} %bitcast_select_fusion.2), channel_id=1, replica_groups=mesh['section'=2,'sy'=8,'sx'=8,'mb'=4] {'sy'}, dimensions={0} | all-to-all | bytes 1572864 | tf_op jit(solution)/shard_map/all_to_all | solution.py:97
  136.3 19.7 %all_to_all.21 = bf16[8,4,8,4,384]{4,3,1,0,2:T(4,128)(2,1)S(1)} all-to-all(bf16[8,4,8,4,384]{4,3,1,0,2:T(4,128)(2,1)S(1)} %copy.53), channel_id=1, replica_groups=mesh['section'=2,'sy'=8,'sx'=8,'mb'=4] {'sx'}, dimensions={2} | all-to-all | bytes 1572864 | tf_op jit(solution)/shard_map/all_to_all | solution.py:96
  158.8 9.2 %collective-permute-done.4 = bf16[32,32,384]{2,1,0:T(8,128)(2,1)S(1)} collective-permute-done((bf16[32,32,384]{2,1,0:T(8,128)(2,1)S(1)}, bf16[32,32,384]{2,1,0:T(8,128)(2,1)S(1)}, u32[]{:S(2)}, u32[]{:S(2)}) %collective-permute-start.4) | collective-permute-done | bytes 786464 | tf_op jit(solution)/shard_map/ppermute | solution.py:25
  168.7 3.8 fusion.13
  175.3 3.3 collective-permute-done.6
  178.6 2.2 collective-permute-start.7
  182.1 3.6 collective-permute-done.8
  189.1 3.9 fusion.24
  193.6 24.2 %all_to_all.22 = bf16[8,4,8,4,384]{4,3,1,2,0:T(4,128)(2,1)S(1)} all-to-all(bf16[8,4,8,4,384]{4,3,1,2,0:T(4,128)(2,1)S(1)} %bitcast_select_fusion.1), channel_id=1, replica_groups=mesh['section'=2,'sy'=8,'sx'=8,'mb'=4] {'sy'}, dimensions={0} | all-to-all | bytes 1572864 | tf_op jit(solution)/shard_map/all_to_all | solution.py:97
  218.9 3.5 all-to-all-start.3
  223.9 2.6 copy.63
  226.5 15.0 %all-to-all-done.3 = bf16[8,4,8,4,384]{4,3,1,0,2:T(4,128)(2,1)S(1)} async-done(((bf16[8,4,8,4,384]{4,3,1,0,2:T(4,128)(2,1)}), bf16[8,4,8,4,384]{4,3,1,0,2:T(4,128)(2,1)S(1)}, u32[]{:S(2)}, u32[]{:S(2)}) %all-to-all-start.3) | async-done | bytes 786464 | tf_op jit(solution)/shard_map/all_to_all | solution.py:96
  247.4 150.4 %all-reduce.5.cloned.1.call-done = f32[384,256]{1,0:T(8,128)} async-done(((f32[384,256]{1,0:T(8,128)}), f32[384,256]{1,0:T(8,128)}) %all-reduce.5.cloned.1.call-update) | async-done | bytes 393232 | tf_op jit(solution)/shard_map/psum | solution.py:133
  399.1 58.8 %psum.30 = f32[]{:T(128)} all-reduce(f32[]{:T(128)S(6)} %select_n.85), channel_id=1, replica_groups=mesh['section'=2,'sy'=8,'sx'=8,'mb'=4] {'sx','mb'}, use_global_device_ids=true, to_apply=%region_11.12 | all-reduce | flops 1 | bytes 8 | tf_op jit(solution)/shard_map/psum | solution.py:133
  457.9 14.6 %psum.31 = f32[]{:T(128)} all-reduce(f32[]{:T(128)} %psum.30), channel_id=1, replica_groups=mesh['section'=2,'sy'=8,'sx'=8,'mb'=4] {'sy'}, use_global_device_ids=true, to_apply=%region_12.13 | all-reduce | flops 1 | bytes 8 | tf_op jit(solution)/shard_map/psum | solution.py:133
  473.3 24.9 %collective-permute-start.10 = (bf16[]{:T(256)}, bf16[]{:T(256)}, u32[]{:S(2)}, u32[]{:S(2)}) collective-permute-start(bf16[]{:T(256)} %convert_element_type.60), channel_id=1, source_target_pairs={{256,0},{257,1},{258,2},{259,3},{260,4},{261,5},{262,6},{263,7},{2... | collective-permute-start | bytes 14 | tf_op jit(solution)/shard_map/ppermute | solution.py:25
  (96 shorter events, 44.3 us)
Async XLA Ops:
  7.2 2.3 copy-start
  7.2 96.1 %all-gather.3.cloned.1.call-start = ((), (), s32[]{:S(2)}) async-start(), calls=%async_computation.6 | async-start | bytes 5391360 | tf_op jit(solution)/shard_map/all_gather | solution.py:81
  15.8 5.3 %collective-permute-start = (bf16[1,32,384]{2,1,0:T(8,128)(2,1)S(1)}, bf16[1,32,384]{2,1,0:T(8,128)(2,1)S(1)}, u32[]{:S(2)}, u32[]{:S(2)}) collective-permute-start(bf16[1,32,384]{2,1,0:T(8,128)(2,1)S(1)} %get-tuple-element.11), channel_id=1, source_target_pairs={{0,32},{32,64},{64,96},{96,128},{128,160},{160,192},{192,224},{1,3... | collective-permute-start | bytes 73736 | tf_op jit(solution)/shard_map/ppermute | solution.py:14
  19.9 4.6 collective-permute-start.1
  24.5 5.3 %collective-permute-start.2 = (bf16[34,1,384]{2,1,0:T(2,128)(2,1)S(1)}, bf16[34,1,384]{2,1,0:T(2,128)(2,1)S(1)}, u32[]{:S(2)}, u32[]{:S(2)}) collective-permute-start(bf16[34,1,384]{2,1,0:T(2,128)(2,1)S(1)} %get-tuple-element.7), channel_id=1, source_target_pairs={{0,4},{4,8},{8,12},{12,16},{16,20},{20,24},{24,28},{1,5},{5,9},{9,... | collective-permute-start | bytes 78344 | tf_op jit(solution)/shard_map/ppermute | solution.py:14
  28.6 5.5 %collective-permute-start.3 = (bf16[34,1,384]{2,1,0:T(2,128)(2,1)S(1)}, bf16[34,1,384]{2,1,0:T(2,128)(2,1)S(1)}, u32[]{:S(2)}, u32[]{:S(2)}) collective-permute-start(bf16[34,1,384]{2,1,0:T(2,128)(2,1)S(1)} %get-tuple-element.8), channel_id=1, source_target_pairs={{4,0},{8,4},{12,8},{16,12},{20,16},{24,20},{28,24},{5,1},{9,5},{13... | collective-permute-start | bytes 78344 | tf_op jit(solution)/shard_map/ppermute | solution.py:17
  157.3 10.7 %collective-permute-start.4 = (bf16[32,32,384]{2,1,0:T(8,128)(2,1)S(1)}, bf16[32,32,384]{2,1,0:T(8,128)(2,1)S(1)}, u32[]{:S(2)}, u32[]{:S(2)}) collective-permute-start(bf16[32,32,384]{2,1,0:T(8,128)(2,1)S(1)} %broadcast_select_fusion), channel_id=1, source_target_pairs={{0,256},{1,257},{2,258},{3,259},{4,260},{5,261},{6,262},{7,263},{8... | collective-permute-start | bytes 2359304 | tf_op jit(solution)/shard_map/ppermute | solution.py:25
  172.6 2.7 collective-permute-start.5
  174.0 4.6 collective-permute-start.6
  178.6 3.5 collective-permute-start.7
  180.8 4.9 collective-permute-start.8
  186.3 2.8 slice-start
  187.3 1.7 slice-start.1
  217.7 5.0 copy-start.3
  218.9 22.6 %all-to-all-start.3 = ((bf16[8,4,8,4,384]{4,3,1,0,2:T(4,128)(2,1)}), bf16[8,4,8,4,384]{4,3,1,0,2:T(4,128)(2,1)S(1)}, u32[]{:S(2)}, u32[]{:S(2)}) async-start(bf16[8,4,8,4,384]{4,3,1,0,2:T(4,128)(2,1)} %copy.58), calls=%async_computation.3 | async-start | bytes 1572864 | tf_op jit(solution)/shard_map/all_to_all | solution.py:96
  222.5 4.0 copy-start.5
  222.5 175.3 %all-reduce.5.cloned.1.call-start = ((), (), s32[]{:S(2)}) async-start(), calls=%async_computation.4 | async-start | bytes 786432 | tf_op jit(solution)/shard_map/psum | solution.py:133
  242.9 1.1 copy-start.2
  244.0 1.2 copy-start.1
  244.0 1.2 copy-start.4
  247.4 250.9 %all-reduce.7.cloned.1.call-start = ((), (), s32[]{:S(2)}) async-start(), calls=%async_computation.5 | async-start | bytes 786432 | tf_op jit(solution)/shard_map/psum | solution.py:133
  473.3 30.6 %collective-permute-start.10 = (bf16[]{:T(256)}, bf16[]{:T(256)}, u32[]{:S(2)}, u32[]{:S(2)}) collective-permute-start(bf16[]{:T(256)} %convert_element_type.60), channel_id=1, source_target_pairs={{256,0},{257,1},{258,2},{259,3},{260,4},{261,5},{262,6},{263,7},{2... | collective-permute-start | bytes 14 | tf_op jit(solution)/shard_map/ppermute | solution.py:25
  501.7 3.0 collective-permute-start.9
Sparse Core Ops, SparseCore 0:
  11.7 91.6 all-gather.2
  247.5 150.2 all-reduce.4
  400.2 75.1 all-reduce.6
